TPU v7x, 32 devices: a whole 2x2x4 slice. The times are simulated.
32 devices in a mesh: frame: 4 (over y, x), row: 8 (over z, core).
Axes of the slice: x: 2, y: 2, z: 4, core: 2. Of those that a mesh axis runs over, the one named last changes fastest.
Arguments:
- residual_in: bfloat16 [4, 8, 64, 768], P('frame', 'row'), may hold values from -6 to 6
- q_spatial: bfloat16 [4, 8, 64, 768], P('frame', 'row'), may hold values from -250 to 250
- k_spatial: bfloat16 [4, 8, 64, 768], P('frame', 'row'), may hold values from -250 to 250
- v_spatial: bfloat16 [4, 8, 64, 768], P('frame', 'row'), may hold values from -6 to 6
- q_temporal: bfloat16 [4, 8, 64, 768], P('frame', 'row'), may hold values from -250 to 250
- k_temporal: bfloat16 [4, 8, 64, 768], P('frame', 'row'), may hold values from -250 to 250
- conv_weight: float32 [3, 3, 768], replicated, may hold values from -2 to 2
- conv_bias: float32 [768], replicated, may hold values from -3 to 3
Outputs:
- spatial_out: bfloat16 [4, 8, 64, 768], P('frame', 'row')
- block_out: bfloat16 [4, 8, 64, 768], P('frame', 'row')
All inputs are finite; a program needn't handle non-finite values.
Results may differ from a plain program's by a relative error of at most 0.0061.
Values may be sent and summed in bfloat16 or wider, within the bound.
A program may use at most 64 MiB of HBM per device.

v0:
```python
import math

import jax
import jax.numpy as jnp
from jax import lax
from jax.sharding import PartitionSpec as P

HEADS = 12
HEAD_DIM = 64


def padded(block, sides, width):
    for axis, dim in sides:
        count = lax.axis_size(axis)
        forward = [(i, i + 1) for i in range(count - 1)]
        backward = [(target, source) for source, target in forward]
        low = lax.ppermute(
            lax.slice_in_dim(block, block.shape[dim] - width, None, axis=dim), axis, forward
        )
        high = lax.ppermute(lax.slice_in_dim(block, 0, width, axis=dim), axis, backward)
        block = jnp.concatenate([low, block, high], axis=dim)
    return block


def absorb(carry_state, query_heads, key_rows, value_rows):
    running_max, running_sum, weighted = carry_state
    scores = jnp.einsum(
        "thd,khd->htk", query_heads, key_rows, preferred_element_type=jnp.float32
    ) * HEAD_DIM ** (-0.5)
    new_max = jnp.maximum(running_max, jnp.max(scores, axis=-1))
    shrink = jnp.exp(running_max - new_max)
    raised = jnp.exp(scores - new_max[..., None])
    running_sum = running_sum * shrink + jnp.sum(raised, axis=-1)
    weighted = weighted * shrink[..., None] + jnp.einsum(
        "htk,khd->htd", raised.astype(jnp.bfloat16), value_rows, preferred_element_type=jnp.float32
    )
    return (new_max, running_sum, weighted)


def frame_attention(queries, keys, values):
    frames, rows_here, across, channels = queries.shape
    shape5 = (frames, rows_here, across, HEADS, HEAD_DIM)
    scores = jnp.einsum(
        "fywhd,gywhd->ywhfg",
        queries.reshape(shape5),
        keys.reshape(shape5),
        preferred_element_type=jnp.float32,
    ) * HEAD_DIM ** (-0.5)
    frame_ids = jnp.arange(frames)
    allowed = frame_ids[:, None] >= frame_ids[None, :]
    scores = jnp.where(allowed, scores, -1e30)
    peak = jnp.max(scores, axis=-1, keepdims=True)
    raised = jnp.exp(scores - peak)
    totals = jnp.sum(raised, axis=-1)
    blended = jnp.einsum(
        "ywhfg,gywhd->fywhd",
        raised.astype(jnp.bfloat16),
        values.reshape(shape5),
        preferred_element_type=jnp.float32,
    )
    blended = blended / jnp.moveaxis(totals, 3, 0)[..., None]
    return blended.reshape(frames, rows_here, across, channels).astype(jnp.bfloat16)


def attend_frames(triple):
    return frame_attention(triple[0], triple[1], triple[2])


def on_device(
    residual_in, q_spatial, k_spatial, v_spatial, q_temporal, k_temporal, conv_weight, conv_bias
):
    rows_here = q_spatial.shape[1]
    across = q_spatial.shape[2]
    tokens_here = rows_here * across
    query_heads = q_spatial.reshape(tokens_here, HEADS, HEAD_DIM)
    start_state = (
        jnp.full((HEADS, tokens_here), -1e30, jnp.float32),
        jnp.zeros((HEADS, tokens_here), jnp.float32),
        jnp.zeros((HEADS, tokens_here, HEAD_DIM), jnp.float32),
    )
    carry_state = start_state
    key_rows = lax.all_gather(k_spatial, "row", axis=1, tiled=True).reshape(-1, HEADS, HEAD_DIM)
    value_rows = lax.all_gather(v_spatial, "row", axis=1, tiled=True).reshape(-1, HEADS, HEAD_DIM)
    length = key_rows.shape[0]
    block = math.gcd(length, 512)
    for begin in range(0, length, block):
        carry_state = absorb(
            carry_state,
            query_heads,
            key_rows[begin : begin + block],
            value_rows[begin : begin + block],
        )
    running_max, running_sum, weighted = carry_state
    attended = weighted / running_sum[..., None]
    spatial_out = jnp.transpose(attended, (1, 0, 2)).reshape(q_spatial.shape).astype(jnp.bfloat16)
    hidden = (residual_in.astype(jnp.float32) + spatial_out.astype(jnp.float32)).astype(
        jnp.bfloat16
    )
    temporal = attend_frames(
        (
            lax.all_to_all(q_temporal, "frame", split_axis=2, concat_axis=0, tiled=True),
            lax.all_to_all(k_temporal, "frame", split_axis=2, concat_axis=0, tiled=True),
            lax.all_to_all(hidden, "frame", split_axis=2, concat_axis=0, tiled=True),
        )
    )
    returned = lax.all_to_all(temporal, "frame", split_axis=0, concat_axis=2, tiled=True)
    mixed = (hidden.astype(jnp.float32) + returned.astype(jnp.float32)).astype(jnp.bfloat16)
    extended = padded(mixed, (("row", 1),), 1)
    widened = jnp.pad(extended, ((0, 0), (0, 0), (1, 1), (0, 0))).astype(jnp.float32)
    conv = jnp.zeros(mixed.shape, jnp.float32) + conv_bias
    for first in range(3):
        for second in range(3):
            conv = (
                conv
                + conv_weight[first, second]
                * widened[:, first : first + rows_here, second : second + across]
            )
    block_out = (mixed.astype(jnp.float32) + jax.nn.gelu(conv)).astype(jnp.bfloat16)
    return (spatial_out, block_out)


def solution(mesh):
    placed = (
        P("frame", "row", None, None),
        P("frame", "row", None, None),
        P("frame", "row", None, None),
        P("frame", "row", None, None),
        P("frame", "row", None, None),
        P("frame", "row", None, None),
        P(),
        P(),
    )
    return jax.shard_map(
        on_device,
        mesh=mesh,
        in_specs=placed,
        out_specs=(P("frame", "row", None, None), P("frame", "row", None, None)),
        check_vma=False,
    )
```

profile of v0, /device:TPU:12, one launch (start us, length us, event | category | flops | bytes accessed | tf_op | source)
XLA Modules:
  0.0 85.7 jit_solution(11516909779274011631)
XLA Ops:
  0.6 1.0 %copy.56 = bf16[1,1,64,768]{3,1,0,2:T(2,128)(2,1)S(1)} copy(bf16[1,1,64,768]{3,2,1,0:T(8,128)(2,1)} %param.13) | data formatting | bytes 196608 | tf_op args[5]
  1.7 0.5 broadcast.79
  2.2 1.1 %reduce.28 = bf16[64,768]{1,0:T(8,128)(2,1)S(1)} reduce(bf16[64,1,1,768]{3,2,1,0:T(2,128)(2,1)S(1)} %bitcast.61, bf16[]{:T(256)} %broadcast.79), dimensions={1,2}, to_apply=%bitcast.58.reduce_sub_computation | reduce | bytes 196610
  3.3 0.7 reshape.173
  4.0 4.2 %all-to-all-start.2 = ((bf16[4,2,6144]{2,1,0:T(2,128)(2,1)}), bf16[4,2,6144]{2,1,0:T(2,128)(2,1)S(1)}, u32[]{:S(2)}, u32[]{:S(2)}) async-start(bf16[4,2,6144]{2,1,0:T(2,128)(2,1)} %reshape.173), calls=%async_computation.2 | async-start | bytes 196608 | tf_op jit(solution)/shard_map/all_to_all | solution.py:102
  8.2 16.0 %all_gather.7 = bf16[1,8,64,768]{3,2,0,1:T(8,128)(2,1)S(1)} all-gather(bf16[1,1,64,768]{3,2,0,1:T(8,128)(2,1)} %bitcast.67), channel_id=1, replica_groups=mesh['frame'=4,'row'=8] {'row'}, dimensions={1}, use_global_device_ids=true | all-gather | bytes 884736 | tf_op jit(solution)/shard_map/all_gather | solution.py:83
  24.2 1.1 %copy.27 = bf16[1,8,64,768]{2,1,3,0:T(8,128)(2,1)S(1)} copy(bf16[1,8,64,768]{3,2,0,1:T(8,128)(2,1)S(1)} %all_gather.7) | data formatting | bytes 1572864 | tf_op jit(solution)/shard_map/all_gather | solution.py:83
  25.3 0.0 copy-start.1
  25.3 1.0 %reshape.156 = bf16[512,12,64]{0,2,1:T(8,128)(2,1)S(1)} reshape(bf16[1,8,64,768]{2,1,3,0:T(8,128)(2,1)S(1)} %copy.27) | data formatting | bytes 1572864 | tf_op jit(solution)/shard_map/reshape | solution.py:83
  26.3 0.0 copy-done.1
  26.3 16.4 %all_gather.6 = bf16[1,8,64,768]{3,2,0,1:T(8,128)(2,1)S(1)} all-gather(bf16[1,1,64,768]{3,2,0,1:T(8,128)(2,1)S(1)} %bitcast.68), channel_id=1, replica_groups=mesh['frame'=4,'row'=8] {'row'}, dimensions={1}, use_global_device_ids=true | all-gather | bytes 884736 | tf_op jit(solution)/shard_map/all_gather | solution.py:82
  42.7 1.1 %copy.24 = bf16[1,8,64,768]{2,1,3,0:T(8,128)(2,1)S(1)} copy(bf16[1,8,64,768]{3,2,0,1:T(8,128)(2,1)S(1)} %all_gather.6) | data formatting | bytes 1572864 | tf_op jit(solution)/shard_map/all_gather | solution.py:82
  43.8 0.0 copy-start.2
  43.8 1.0 %reshape.155 = bf16[512,12,64]{0,2,1:T(8,128)(2,1)S(1)} reshape(bf16[1,8,64,768]{2,1,3,0:T(8,128)(2,1)S(1)} %copy.24) | data formatting | bytes 1572864 | tf_op jit(solution)/shard_map/reshape | solution.py:82
  44.8 0.0 copy-done.2
  44.8 0.2 reshape.154
  45.0 0.4 fusion.44
  45.4 0.6 fusion
  46.0 0.0 copy-start.3
  46.0 0.5 fusion.5
  46.5 0.0 copy-start.4
  46.6 0.1 copy.28
  46.7 0.2 convert_element_type.89
  46.9 0.0 copy-done.3
  46.9 0.0 copy-start
  46.9 0.2 copy.57
  47.1 1.1 %reduce.29 = bf16[64,768]{1,0:T(8,128)(2,1)S(1)} reduce(bf16[64,1,1,768]{3,2,1,0:T(2,128)(2,1)S(1)} %bitcast.63, bf16[]{:T(256)} %broadcast.79), dimensions={1,2}, to_apply=%bitcast.59.reduce_sub_computation | reduce | bytes 196610
  48.2 0.6 reshape.175
  48.8 0.0 copy-done.4
  48.9 0.2 copy.58
  49.0 1.1 %reduce.30 = bf16[64,768]{1,0:T(8,128)(2,1)S(1)} reduce(bf16[64,1,1,768]{3,2,1,0:T(2,128)(2,1)S(1)} %bitcast.62, bf16[]{:T(256)} %broadcast.79), dimensions={1,2}, to_apply=%bitcast.60.reduce_sub_computation | reduce | bytes 196610
  50.1 0.7 reshape.177
  50.8 0.0 all-to-all-done.2
  50.8 4.2 %all-to-all-start.1 = ((bf16[4,2,6144]{2,1,0:T(2,128)(2,1)}), bf16[4,2,6144]{2,1,0:T(2,128)(2,1)S(1)}, u32[]{:S(2)}, u32[]{:S(2)}) async-start(bf16[4,2,6144]{2,1,0:T(2,128)(2,1)} %reshape.175), calls=%async_computation.1 | async-start | bytes 196608 | tf_op jit(solution)/shard_map/all_to_all | solution.py:101
  55.0 0.1 reshape.174
  55.1 0.5 bitcast_reduce_fusion.2
  55.7 0.2 reshape.159
  55.8 2.9 %all-to-all-done.1 = bf16[4,2,6144]{2,1,0:T(2,128)(2,1)S(1)} async-done(((bf16[4,2,6144]{2,1,0:T(2,128)(2,1)}), bf16[4,2,6144]{2,1,0:T(2,128)(2,1)S(1)}, u32[]{:S(2)}, u32[]{:S(2)}) %all-to-all-start.1) | async-done | bytes 98336 | tf_op jit(solution)/shard_map/all_to_all | solution.py:101
  58.8 0.0 copy-done
  58.8 4.5 %all-to-all-start = ((bf16[4,2,6144]{2,1,0:T(2,128)(2,1)}), bf16[4,2,6144]{2,1,0:T(2,128)(2,1)S(1)}, u32[]{:S(2)}, u32[]{:S(2)}) async-start(bf16[4,2,6144]{2,1,0:T(2,128)(2,1)} %reshape.177), calls=%async_computation | async-start | bytes 196608 | tf_op jit(solution)/shard_map/all_to_all | solution.py:103
  63.2 0.1 reshape.176
  63.3 0.5 bitcast_reduce_fusion.1
  63.9 0.2 reshape.158
  64.0 2.9 %all-to-all-done = bf16[4,2,6144]{2,1,0:T(2,128)(2,1)S(1)} async-done(((bf16[4,2,6144]{2,1,0:T(2,128)(2,1)}), bf16[4,2,6144]{2,1,0:T(2,128)(2,1)S(1)}, u32[]{:S(2)}, u32[]{:S(2)}) %all-to-all-start) | async-done | bytes 98336 | tf_op jit(solution)/shard_map/all_to_all | solution.py:103
  67.0 0.1 reshape.178
  67.1 0.5 bitcast_reduce_fusion
  67.6 0.2 reshape.157
  67.8 0.5 fusion.45
  68.3 0.3 fusion.17
  68.7 0.0 copy-start.5
  68.7 0.5 fusion.7
  69.2 0.0 copy-start.6
  69.3 0.2 convert_element_type.96
  69.4 7.3 %all_to_all.16 = bf16[4,1,16,768]{3,2,1,0:T(8,128)(2,1)S(1)} all-to-all(bf16[4,1,16,768]{3,2,1,0:T(8,128)(2,1)S(1)} %bitcast.65), channel_id=1, replica_groups=mesh['frame'=4,'row'=8] {'frame'}, dimensions={0} | all-to-all | bytes 196608 | tf_op jit(solution)/shard_map/all_to_all | solution.py:106
  76.8 1.9 %collective-permute-start.1 = (bf16[1,1,64,768]{3,2,1,0:T(8,128)(2,1)S(1)}, bf16[1,1,64,768]{3,2,1,0:T(8,128)(2,1)S(1)}, u32[]{:S(2)}, u32[]{:S(2)}) collective-permute-start(bf16[1,1,64,768]{3,2,1,0:T(8,128)(2,1)S(1)} %fusion.38), channel_id=1, source_target_pairs={{1,0},{2,1},{3,2},{4,3},{5,4},{6,5},{7,6},{9,8},{10,9},{11,10},{12... | collective-permute-start | bytes 294920 | tf_op jit(solution)/shard_map/ppermute | solution.py:20
  78.7 2.4 %collective-permute-start = (bf16[1,1,64,768]{3,2,1,0:T(8,128)(2,1)S(1)}, bf16[1,1,64,768]{3,2,1,0:T(8,128)(2,1)S(1)}, u32[]{:S(2)}, u32[]{:S(2)}) collective-permute-start(bf16[1,1,64,768]{3,2,1,0:T(8,128)(2,1)S(1)} %fusion.38), channel_id=1, source_target_pairs={{0,1},{1,2},{2,3},{3,4},{4,5},{5,6},{6,7},{8,9},{9,10},{10,11},{11... | collective-permute-start | bytes 294920 | tf_op jit(solution)/shard_map/ppermute | solution.py:17
  81.1 0.0 copy-done.5
  81.1 0.1 slice_reduce_fusion.8
  81.2 0.0 collective-permute-done.1
  81.2 3.4 %collective-permute-done = bf16[1,1,64,768]{3,2,1,0:T(8,128)(2,1)S(1)} collective-permute-done((bf16[1,1,64,768]{3,2,1,0:T(8,128)(2,1)S(1)}, bf16[1,1,64,768]{3,2,1,0:T(8,128)(2,1)S(1)}, u32[]{:S(2)}, u32[]{:S(2)}) %collective-permute-start) | collective-permute-done | bytes 98336 | tf_op jit(solution)/shard_map/ppermute | solution.py:17
  84.6 0.1 fusion.16
  84.7 0.0 copy-done.6
  84.7 0.9 %fusion.27 = bf16[1,1,64,768]{3,2,1,0:T(8,128)(2,1)} fusion(f32[1,3,66,768]{3,2,1,0:T(8,128)S(1)} %fusion.16, bf16[1,1,64,768]{3,2,1,0:T(8,128)(2,1)S(1)} %fusion.38, f32[768]{0:T(1024)S(1)} %get-tuple-element.9, f32[768]{0:T(1024)S(1)} %get-tuple-element.10, f32[768]{0:T(1024)S(1)} %get-tuple-element.3, f32[768]{0:T(1024)S(1)} %get-tuple-element.4, ...), kind=kLoop, calls=%fused_computation.35 | loop fusion | flops 1425408 | bytes 1996800 | tf_op jit(solution)/shard_map/convert_element_type | solution.py:118
  (6 shorter events, 0.1 us)
Async XLA Ops:
  4.0 46.8 %all-to-all-start.2 = ((bf16[4,2,6144]{2,1,0:T(2,128)(2,1)}), bf16[4,2,6144]{2,1,0:T(2,128)(2,1)S(1)}, u32[]{:S(2)}, u32[]{:S(2)}) async-start(bf16[4,2,6144]{2,1,0:T(2,128)(2,1)} %reshape.173), calls=%async_computation.2 | async-start | bytes 196608 | tf_op jit(solution)/shard_map/all_to_all | solution.py:102
  25.3 1.0 %copy-start.1 = (bf16[1,1,64,768]{3,2,1,0:T(8,128)(2,1)S(1)}, bf16[1,1,64,768]{3,2,1,0:T(8,128)(2,1)}, u32[]{:S(2)}) copy-start(bf16[1,1,64,768]{3,2,1,0:T(8,128)(2,1)} %param.10) | copy-start | bytes 294916
  43.8 1.0 %copy-start.2 = (bf16[1,1,64,768]{3,2,1,0:T(8,128)(2,1)S(1)}, bf16[1,1,64,768]{3,2,1,0:T(8,128)(2,1)}, u32[]{:S(2)}) copy-start(bf16[1,1,64,768]{3,2,1,0:T(8,128)(2,1)} %param.9) | copy-start | bytes 294916
  46.0 0.9 %copy-start.3 = (bf16[1,1,64,768]{3,2,1,0:T(8,128)(2,1)S(1)}, bf16[1,1,64,768]{3,2,1,0:T(8,128)(2,1)}, u32[]{:S(2)}) copy-start(bf16[1,1,64,768]{3,2,1,0:T(8,128)(2,1)} %param.12) | copy-start | bytes 294916
  46.5 2.3 %copy-start.4 = (bf16[1,1,64,768]{3,2,1,0:T(8,128)(2,1)S(1)}, bf16[1,1,64,768]{3,2,1,0:T(8,128)(2,1)}, u32[]{:S(2)}) copy-start(bf16[1,1,64,768]{3,2,1,0:T(8,128)(2,1)} %param.8) | copy-start | bytes 294916
  46.9 11.9 %copy-start = (bf16[1,1,64,768]{3,2,1,0:T(8,128)(2,1)}, bf16[1,1,64,768]{3,2,1,0:T(8,128)(2,1)S(1)}, u32[]{:S(2)}) copy-start(bf16[1,1,64,768]{3,2,1,0:T(8,128)(2,1)S(1)} %convert_element_type.89) | copy-start | bytes 294916
  50.8 7.9 %all-to-all-start.1 = ((bf16[4,2,6144]{2,1,0:T(2,128)(2,1)}), bf16[4,2,6144]{2,1,0:T(2,128)(2,1)S(1)}, u32[]{:S(2)}, u32[]{:S(2)}) async-start(bf16[4,2,6144]{2,1,0:T(2,128)(2,1)} %reshape.175), calls=%async_computation.1 | async-start | bytes 196608 | tf_op jit(solution)/shard_map/all_to_all | solution.py:101
  58.8 8.2 %all-to-all-start = ((bf16[4,2,6144]{2,1,0:T(2,128)(2,1)}), bf16[4,2,6144]{2,1,0:T(2,128)(2,1)S(1)}, u32[]{:S(2)}, u32[]{:S(2)}) async-start(bf16[4,2,6144]{2,1,0:T(2,128)(2,1)} %reshape.177), calls=%async_computation | async-start | bytes 196608 | tf_op jit(solution)/shard_map/all_to_all | solution.py:103
  68.7 12.5 %copy-start.5 = (f32[3,3,768]{2,1,0:T(4,128)S(1)}, f32[3,3,768]{2,1,0:T(4,128)}, u32[]{:S(2)}) copy-start(f32[3,3,768]{2,1,0:T(4,128)} %param.14) | copy-start | bytes 82948
  69.2 15.5 %copy-start.6 = (f32[768]{0:T(1024)S(1)}, f32[768]{0:T(1024)}, u32[]{:S(2)}) copy-start(f32[768]{0:T(1024)} %param.15) | copy-start | bytes 9220
  76.8 4.4 %collective-permute-start.1 = (bf16[1,1,64,768]{3,2,1,0:T(8,128)(2,1)S(1)}, bf16[1,1,64,768]{3,2,1,0:T(8,128)(2,1)S(1)}, u32[]{:S(2)}, u32[]{:S(2)}) collective-permute-start(bf16[1,1,64,768]{3,2,1,0:T(8,128)(2,1)S(1)} %fusion.38), channel_id=1, source_target_pairs={{1,0},{2,1},{3,2},{4,3},{5,4},{6,5},{7,6},{9,8},{10,9},{11,10},{12... | collective-permute-start | bytes 294920 | tf_op jit(solution)/shard_map/ppermute | solution.py:20
  78.7 5.9 %collective-permute-start = (bf16[1,1,64,768]{3,2,1,0:T(8,128)(2,1)S(1)}, bf16[1,1,64,768]{3,2,1,0:T(8,128)(2,1)S(1)}, u32[]{:S(2)}, u32[]{:S(2)}) collective-permute-start(bf16[1,1,64,768]{3,2,1,0:T(8,128)(2,1)S(1)} %fusion.38), channel_id=1, source_target_pairs={{0,1},{1,2},{2,3},{3,4},{4,5},{5,6},{6,7},{8,9},{9,10},{10,11},{11... | collective-permute-start | bytes 294920 | tf_op jit(solution)/shard_map/ppermute | solution.py:17
where the time goes:
time: 87.2 us; the launch traced here: 85.7 us
  blocking collectives  39.7 us (46%)
  starting transfers between devices  17.2 us (20%)
  local copies, waits for them, and re-layouts  11.2 us (13%)
  waiting for transfers between devices  9.27 us (11%)
  other arithmetic  5.33 us (6%)
  matrix products  2.02 us (2%)
  between operations  0.96 us (1%)
    all_gather x1, blocking collectives, on_device(): lax.all_gather(k_spatial, 'row', axis=1, tiled=True)  16.4 us
    all_gather x1, blocking collectives, on_device(): lax.all_gather(v_spatial, 'row', axis=1, tiled=True)  16 us
    all_to_all x1, blocking collectives, on_device(): lax.all_to_all(temporal, 'frame', split_axis=0, concat_axis=2, tiled=True)  7.31 us
    all_to_all x1, starting transfers between devices, on_device(): lax.all_to_all(hidden, 'frame', split_axis=2, concat_axis=0, tiled=True)  4.47 us
    all_to_all x1, starting transfers between devices, on_device(): lax.all_to_all(k_temporal, 'frame', split_axis=2, concat_axis=0, tiled=True)  4.22 us
    all_to_all x1, starting transfers between devices, on_device(): lax.all_to_all(q_temporal, 'frame', split_axis=2, concat_axis=0, tiled=True)  4.2 us
    unnamed x23, local copies, waits for them, and re-layouts  4.01 us
    ppermute x1, waiting for transfers between devices, padded(): lax.ppermute(lax.slice_in_dim(block, block.shape[dim] - width, None, axis...  3.42 us
  transfers between devices with their start and end apart: 5, of which 3 were waited for; matrix products, arithmetic and copies ran while one was open for 14% of the time, Pallas kernels for 0%

commit v1 on v0

v1 whole, which is shorter than its diff:
```python
import functools
import math

import jax
import jax.numpy as jnp
from jax import lax
from jax.experimental import pallas as pl
from jax.experimental.pallas import tpu as pltpu
from jax.sharding import PartitionSpec as P

HEAD_DIM = 64
LANES = 2 * HEAD_DIM
SCALE = HEAD_DIM ** (-0.5)
LOG2E = math.log2(math.e)


def block_kernel(
    frames, rows, chunks, tokens,
    res_hbm, q_hbm, k_hbm, v_hbm, qt_hbm, kt_hbm, cw_hbm, cb_hbm,
    so_hbm, bo_hbm,
    kv, qs, rs, qts, ktb, hb, tsc, wts, peak, rden, mixb, sob, bob, cwv, cbv,
    ld_kv, ld_misc, kv_recv, up_send, dn_send, pt_send,
    kt_recv, kt_send, h_recv, h_send, halo_recv, halo_send, out_sem,
):
    me_f = lax.axis_index("frame")
    me_r = lax.axis_index("row")
    chips = rows // 2
    z = me_r // 2
    core = me_r % 2

    def lanes(c):
        return pl.ds(c * LANES, LANES)

    for c in range(chunks):
        pltpu.make_async_copy(k_hbm.at[0, 0, :, lanes(c)], kv.at[me_r, c, 0], ld_kv.at[c]).start()
        pltpu.make_async_copy(v_hbm.at[0, 0, :, lanes(c)], kv.at[me_r, c, 1], ld_kv.at[c]).start()
    for c in range(chunks):
        pltpu.make_async_copy(kt_hbm.at[0, 0, :, lanes(c)], ktb.at[me_f, c], ld_misc.at[0]).start()
    for c in range(chunks):
        pltpu.make_async_copy(qt_hbm.at[0, 0, :, lanes(c)], qts.at[c], ld_misc.at[1]).start()
        pltpu.make_async_copy(q_hbm.at[0, 0, :, lanes(c)], qs.at[c], ld_misc.at[2]).start()
        pltpu.make_async_copy(res_hbm.at[0, 0, :, lanes(c)], rs.at[c], ld_misc.at[3]).start()
    pltpu.make_async_copy(cw_hbm, cwv, ld_misc.at[4]).start()
    pltpu.make_async_copy(cb_hbm, cbv, ld_misc.at[5]).start()

    barrier = pltpu.get_barrier_semaphore()

    def greet(**where):
        pl.semaphore_signal(
            barrier, inc=1, device_id=where, device_id_type=pl.DeviceIdType.MESH
        )

    greet(row=me_r + 1 - 2 * core)

    @pl.when(z > 0)
    def _():
        greet(row=me_r - 2)

    @pl.when(z < chips - 1)
    def _():
        greet(row=me_r + 2)

    across = me_r - 1 + 2 * core
    has_across = jnp.logical_and(across >= 0, across < rows)

    @pl.when(has_across)
    def _():
        greet(row=across)

    @pl.loop(1, frames)
    def _(step):
        greet(frame=(me_f + step) % frames)

    pl.semaphore_wait(
        barrier,
        frames
        + (z > 0).astype(jnp.int32)
        + (z < chips - 1).astype(jnp.int32)
        + has_across.astype(jnp.int32),
    )

    def remote(src, dst, send, recv, **where):
        return pltpu.make_async_remote_copy(
            src_ref=src, dst_ref=dst, send_sem=send, recv_sem=recv,
            device_id=where, device_id_type=pl.DeviceIdType.MESH,
        )

    def kv_copy(chip, of_core, c, send, to_row):
        src = 2 * chip + of_core
        return remote(kv.at[src, c], kv.at[src, c], send, kv_recv.at[src, c], row=to_row)

    def go_up(chip, c):
        return kv_copy(chip, core, c, up_send.at[chip, c], me_r + 2)

    def go_down(chip, c):
        return kv_copy(chip, core, c, dn_send.at[chip, c], me_r - 2)

    def to_partner(chip, c):
        return kv_copy(chip, core, c, pt_send.at[chip, c], me_r + 1 - 2 * core)

    def wait_slot(chip, of_core, c):
        kv_copy(chip, of_core, c, up_send.at[chip, c], me_r + 1 - 2 * core).wait_recv()

    def kt_copy(g, to):
        return remote(ktb.at[g], ktb.at[g], kt_send.at[to], kt_recv.at[g], frame=to)

    def h_copy(g, to, c):
        return remote(hb.at[g, c], hb.at[g, c], h_send.at[to, c], h_recv.at[g, c], frame=to)

    def halo_copy(side, c):
        return remote(
            mixb.at[1, c], mixb.at[2 - 2 * side, c], halo_send.at[side, c],
            halo_recv.at[1 - side, c], row=me_r - 1 + 2 * side,
        )

    for c in range(chunks):
        pltpu.make_async_copy(kv.at[me_r, c], kv.at[me_r, c], ld_kv.at[c]).wait()

        @pl.when(z > 0)
        def _(c=c):
            go_down(z, c).start()

        @pl.when(z < chips - 1)
        def _(c=c):
            go_up(z, c).start()

        to_partner(z, c).start()

    pltpu.make_async_copy(ktb.at[me_f], ktb.at[me_f], ld_misc.at[0]).wait()

    @pl.loop(me_f + 1, frames)
    def _(to):
        kt_copy(me_f, to).start()

    def relay(d, c):
        @pl.when(z - d >= 0)
        def _():
            wait_slot(z - d, core, c)

            @pl.when(z < chips - 1)
            def _():
                go_up(z - d, c).start()

            to_partner(z - d, c).start()

        @pl.when(z + d < chips)
        def _():
            wait_slot(z + d, core, c)

            @pl.when(z > 0)
            def _():
                go_down(z + d, c).start()

            to_partner(z + d, c).start()

    @pl.loop(1, chips - 1)
    def _(d):
        for c in range(chunks):
            relay(d, c)

    pltpu.make_async_copy(qts, qts, ld_misc.at[1]).wait()

    @pl.loop(0, me_f)
    def _(g):
        kt_copy(g, me_f).wait_recv()

    flat = chunks * tokens
    same = (
        (lax.broadcasted_iota(jnp.int32, (2 * LANES, LANES), 0) // HEAD_DIM) % 2
        == lax.broadcasted_iota(jnp.int32, (2 * LANES, LANES), 1) // HEAD_DIM
    )
    spread = jnp.where(same, 1.0, 0.0).astype(jnp.bfloat16)
    peak[...] = jnp.full(peak.shape, -1e30, jnp.float32)

    @pl.loop(0, me_f + 1)
    def _(g):
        product = (
            qts[...].reshape(flat, LANES).astype(jnp.float32)
            * ktb[g].reshape(flat, LANES).astype(jnp.float32)
        )
        high = product.astype(jnp.bfloat16)
        low = (product - high.astype(jnp.float32)).astype(jnp.bfloat16)
        score = jnp.dot(
            jnp.concatenate([high, low], axis=1), spread, preferred_element_type=jnp.float32
        )
        tsc[g] = score
        peak[...] = jnp.maximum(peak[...], score)

    rden[...] = jnp.zeros(rden.shape, jnp.float32)

    @pl.loop(0, me_f + 1)
    def _(g):
        raised = jnp.exp2((tsc[g] - peak[...]) * (SCALE * LOG2E))
        rden[...] += raised
        wts[g] = raised.astype(jnp.bfloat16)

    rden[...] = 1.0 / rden[...]

    pltpu.make_async_copy(qs, qs, ld_misc.at[2]).wait()
    pltpu.make_async_copy(rs, rs, ld_misc.at[3]).wait()

    first_head = lax.broadcasted_iota(jnp.int32, (tokens, LANES), 1) < HEAD_DIM
    keys = rows * tokens

    for c in range(chunks):
        relay(chips - 1, c)

        @pl.loop(0, chips)
        def _(chip, c=c):
            wait_slot(chip, 1 - core, c)

        q = qs[c]
        none = jnp.zeros_like(q)
        q2 = jnp.concatenate(
            [jnp.where(first_head, q, none), jnp.where(first_head, none, q)], axis=0
        )
        scores = lax.dot_general(
            q2, kv[:, c, 0].reshape(keys, LANES), (((1,), (1,)), ((), ())),
            preferred_element_type=jnp.float32,
        )
        top = jnp.max(scores, axis=1, keepdims=True)
        raised = jnp.exp2((scores - top) * (SCALE * LOG2E))
        denom = jnp.sum(raised, axis=1, keepdims=True)
        both = jnp.dot(
            raised.astype(jnp.bfloat16), kv[:, c, 1].reshape(keys, LANES),
            preferred_element_type=jnp.float32,
        ) / denom
        spatial = jnp.where(first_head, both[:tokens], both[tokens:]).astype(jnp.bfloat16)
        sob[c] = spatial
        hb[me_f, c] = (rs[c].astype(jnp.float32) + spatial.astype(jnp.float32)).astype(jnp.bfloat16)

        @pl.loop(me_f + 1, frames)
        def _(to, c=c):
            h_copy(me_f, to, c).start()

        pltpu.make_async_copy(sob.at[c], so_hbm.at[0, 0, :, lanes(c)], out_sem.at[0]).start()

    for c in range(chunks):
        @pl.loop(0, me_f)
        def _(g, c=c):
            h_copy(g, me_f, c).wait_recv()

        here = pl.ds(c * tokens, tokens)

        def add(g, total):
            return total + wts[g, here].astype(jnp.float32) * hb[g, c].astype(jnp.float32)

        total = lax.fori_loop(0, me_f + 1, add, jnp.zeros((tokens, LANES), jnp.float32))
        temporal = (total * rden[here]).astype(jnp.bfloat16)
        mixb[1, c] = (
            hb[me_f, c].astype(jnp.float32) + temporal.astype(jnp.float32)
        ).astype(jnp.bfloat16)

        @pl.when(me_r > 0)
        def _(c=c):
            halo_copy(0, c).start()

        @pl.when(me_r < rows - 1)
        def _(c=c):
            halo_copy(1, c).start()

    pltpu.make_async_copy(cwv, cwv, ld_misc.at[4]).wait()
    pltpu.make_async_copy(cbv, cbv, ld_misc.at[5]).wait()

    @pl.when(me_r == 0)
    def _():
        mixb[0] = jnp.zeros(mixb.shape[1:], mixb.dtype)

    @pl.when(me_r == rows - 1)
    def _():
        mixb[2] = jnp.zeros(mixb.shape[1:], mixb.dtype)

    position = lax.broadcasted_iota(jnp.int32, (tokens, LANES), 0)
    for c in range(chunks):
        @pl.when(me_r > 0)
        def _(c=c):
            remote(
                mixb.at[0, c], mixb.at[0, c], halo_send.at[0, c], halo_recv.at[0, c],
                row=me_r - 1,
            ).wait_recv()

        @pl.when(me_r < rows - 1)
        def _(c=c):
            remote(
                mixb.at[2, c], mixb.at[2, c], halo_send.at[1, c], halo_recv.at[1, c],
                row=me_r + 1,
            ).wait_recv()

        lines = [mixb[a, c].astype(jnp.float32) for a in range(3)]
        taps = [
            sum(cwv[a, pl.ds(b, 1), lanes(c)] * lines[a] for a in range(3)) for b in range(3)
        ]
        left = jnp.where(position == 0, 0.0, pltpu.roll(taps[0], 1, 0))
        right = jnp.where(position == tokens - 1, 0.0, pltpu.roll(taps[2], tokens - 1, 0))
        conv = cbv[pl.ds(c * LANES, LANES)].reshape(1, LANES) + taps[1] + left + right
        inner = math.sqrt(2.0 / math.pi) * (conv + 0.044715 * (conv * conv * conv))
        bob[c] = (lines[1] + 0.5 * conv * (1.0 + jnp.tanh(inner))).astype(jnp.bfloat16)
        pltpu.make_async_copy(bob.at[c], bo_hbm.at[0, 0, :, lanes(c)], out_sem.at[1]).start()

    @pl.loop(0, chips)
    def _(chip):
        for c in range(chunks):
            to_partner(chip, c).wait_send()

            @pl.when(jnp.logical_and(chip <= z, z < chips - 1))
            def _(c=c):
                go_up(chip, c).wait_send()

            @pl.when(jnp.logical_and(chip >= z, z > 0))
            def _(c=c):
                go_down(chip, c).wait_send()

    @pl.loop(me_f + 1, frames)
    def _(to):
        kt_copy(me_f, to).wait_send()
        for c in range(chunks):
            h_copy(me_f, to, c).wait_send()

    for c in range(chunks):
        @pl.when(me_r > 0)
        def _(c=c):
            halo_copy(0, c).wait_send()

        @pl.when(me_r < rows - 1)
        def _(c=c):
            halo_copy(1, c).wait_send()

    pltpu.make_async_copy(sob, sob, out_sem.at[0]).wait()
    pltpu.make_async_copy(bob, bob, out_sem.at[1]).wait()


def on_device(frames, rows, *args):
    block = args[0]
    _, _, tokens, channels = block.shape
    chunks = channels // LANES
    chips = rows // 2
    slab = (chunks, tokens, LANES)
    flat = (chunks * tokens, LANES)
    bf16, f32 = jnp.bfloat16, jnp.float32
    dma = pltpu.SemaphoreType.DMA
    anywhere = pl.BlockSpec(memory_space=pl.ANY)
    return pl.pallas_call(
        functools.partial(block_kernel, frames, rows, chunks, tokens),
        out_shape=(jax.ShapeDtypeStruct(block.shape, bf16),) * 2,
        in_specs=[anywhere] * 8,
        out_specs=(anywhere, anywhere),
        scratch_shapes=[
            pltpu.VMEM((rows, chunks, 2, tokens, LANES), bf16),
            pltpu.VMEM(slab, bf16),
            pltpu.VMEM(slab, bf16),
            pltpu.VMEM(slab, bf16),
            pltpu.VMEM((frames,) + slab, bf16),
            pltpu.VMEM((frames,) + slab, bf16),
            pltpu.VMEM((frames,) + flat, f32),
            pltpu.VMEM((frames,) + flat, bf16),
            pltpu.VMEM(flat, f32),
            pltpu.VMEM(flat, f32),
            pltpu.VMEM((3,) + slab, bf16),
            pltpu.VMEM(slab, bf16),
            pltpu.VMEM(slab, bf16),
            pltpu.VMEM(args[6].shape, f32),
            pltpu.VMEM(args[7].shape, f32),
            dma((chunks,)), dma((6,)), dma((rows, chunks)),
            dma((chips, chunks)), dma((chips, chunks)), dma((chips, chunks)),
            dma((frames,)), dma((frames,)), dma((frames, chunks)), dma((frames, chunks)),
            dma((2, chunks)), dma((2, chunks)), dma((2,)),
        ],
        compiler_params=pltpu.CompilerParams(collective_id=0, has_side_effects=True),
        name="block",
    )(*args)


def solution(mesh):
    split = P("frame", "row", None, None)
    return jax.shard_map(
        functools.partial(on_device, mesh.shape["frame"], mesh.shape["row"]),
        mesh=mesh,
        in_specs=(split,) * 6 + (P(), P()),
        out_specs=(split, split),
        check_vma=False,
    )
```

time: 87.2 us -> 33.6 us (0.39)
  the two profiles are of different devices: /device:TPU:12 before, /device:TPU:23 now
where the time goes in v1:
time: 33.6 us; the launch traced here: 33.4 us
  Pallas kernels  30.6 us (91%)
  local copies, waits for them, and re-layouts  2.22 us (7%)
  between operations  0.65 us (2%)
    pallas_call x1, Pallas kernels, on_device(): pl.pallas_call(functools.partial(block_kernel, frames, rows, chunks, toke...  30.6 us
    unnamed x4, local copies, waits for them, and re-layouts  2.22 us

profile of v1, /device:TPU:23, one launch (start us, length us, event | category | flops | bytes accessed | tf_op | source)
XLA Modules:
  0.0 33.4 jit_solution(4048800619782857156)
XLA Ops:
  0.6 30.6 %block.1 = (bf16[1,1,64,768]{3,2,1,0:T(8,128)(2,1)}, bf16[1,1,64,768]{3,2,1,0:T(8,128)(2,1)}) custom-call(bf16[1,1,64,768]{3,2,1,0:T(8,128)(2,1)} %res_hbm.1, bf16[1,1,64,768]{3,2,1,0:T(8,128)(2,1)} %q_hbm.1, bf16[1,1,64,768]{3,2,1,0:T(8,128)(2,1)} %k_hbm.1, bf16[1,1,64,768]{3,2,1,0:T(8,128)(2,1)} %v_hbm.1, bf16[1,1,64,768]{3,2,1,0:T(8,128)(2,1)} %qt_hbm.1, ...), custom_call_target="tpu_custom_call" | custom-call | tf_op jit(solution)/shard_map/block/pallas_call | solution.py:342
  31.2 0.0 copy-start
  31.2 1.6 %copy.12 = bf16[1,1,64,768]{3,2,1,0:T(8,128)(2,1)} copy(bf16[1,1,64,768]{3,2,1,0:T(8,128)(2,1)} %get-tuple-element.4) | data formatting | bytes 196608
  32.8 0.0 copy-done
  32.8 0.6 %copy.13 = bf16[1,1,64,768]{3,2,1,0:T(8,128)(2,1)} copy(bf16[1,1,64,768]{3,2,1,0:T(8,128)(2,1)S(1)} %copy-done) | data formatting | bytes 196608
Async XLA Ops:
  31.2 1.6 %copy-start = (bf16[1,1,64,768]{3,2,1,0:T(8,128)(2,1)S(1)}, bf16[1,1,64,768]{3,2,1,0:T(8,128)(2,1)}, u32[]{:S(2)}) copy-start(bf16[1,1,64,768]{3,2,1,0:T(8,128)(2,1)} %get-tuple-element.5) | copy-start | bytes 294916

commit v2 on v1

--- a/solution.py
+++ b/solution.py
@@ -15,18 +15,30 @@
 
 
 def block_kernel(
-    frames, rows, chunks, tokens,
+    frames, rows, chunks, tokens, lent,
     res_hbm, q_hbm, k_hbm, v_hbm, qt_hbm, kt_hbm, cw_hbm, cb_hbm,
     so_hbm, bo_hbm,
-    kv, qs, rs, qts, ktb, hb, tsc, wts, peak, rden, mixb, sob, bob, cwv, cbv,
+    kv, qs, qh, oh, rs, qts, ktb, hb, tsc, wts, peak, rden, mixb, sob, bob, cwv, cbv,
     ld_kv, ld_misc, kv_recv, up_send, dn_send, pt_send,
-    kt_recv, kt_send, h_recv, h_send, halo_recv, halo_send, out_sem,
+    kt_recv, kt_send, h_recv, h_send, halo_recv, halo_send, out_sem, lend_sem, give_sem, back_sem,
 ):
     me_f = lax.axis_index("frame")
     me_r = lax.axis_index("row")
     chips = rows // 2
     z = me_r // 2
     core = me_r % 2
+    at_end = jnp.logical_or(z == 0, z == chips - 1)
+    helps = jnp.logical_or(z == 1, z == chips - 2)
+    mate = me_r + 2 * jnp.where(jnp.logical_or(z == 0, z == chips - 2), 1, -1)
+
+    def has_up(c):
+        return z < chips - 1 - (1 if c < lent else 0)
+
+    def has_down(c):
+        return z > (1 if c < lent else 0)
+
+    def attends(c):
+        return jnp.logical_not(at_end) if c < lent else z >= 0
 
     def lanes(c):
         return pl.ds(c * LANES, LANES)
@@ -113,18 +125,32 @@
             halo_recv.at[1 - side, c], row=me_r - 1 + 2 * side,
         )
 
+    def lend():
+        return remote(qs.at[pl.ds(0, lent)], qh, lend_sem.at[0], lend_sem.at[1], row=mate)
+
+    def give_back(c):
+        return remote(oh.at[c], sob.at[c], give_sem.at[c], back_sem.at[c], row=mate)
+
     for c in range(chunks):
         pltpu.make_async_copy(kv.at[me_r, c], kv.at[me_r, c], ld_kv.at[c]).wait()
 
-        @pl.when(z > 0)
+        @pl.when(has_down(c))
         def _(c=c):
             go_down(z, c).start()
 
-        @pl.when(z < chips - 1)
+        @pl.when(has_up(c))
         def _(c=c):
             go_up(z, c).start()
 
-        to_partner(z, c).start()
+        @pl.when(attends(c))
+        def _(c=c):
+            to_partner(z, c).start()
+
+    pltpu.make_async_copy(qs, qs, ld_misc.at[2]).wait()
+    if lent:
+        @pl.when(at_end)
+        def _():
+            lend().start()
 
     pltpu.make_async_copy(ktb.at[me_f], ktb.at[me_f], ld_misc.at[0]).wait()
 
@@ -133,21 +159,21 @@
         kt_copy(me_f, to).start()
 
     def relay(d, c):
-        @pl.when(z - d >= 0)
+        @pl.when(jnp.logical_and(z - d >= 0, attends(c)))
         def _():
             wait_slot(z - d, core, c)
 
-            @pl.when(z < chips - 1)
+            @pl.when(has_up(c))
             def _():
                 go_up(z - d, c).start()
 
             to_partner(z - d, c).start()
 
-        @pl.when(z + d < chips)
+        @pl.when(jnp.logical_and(z + d < chips, attends(c)))
         def _():
             wait_slot(z + d, core, c)
 
-            @pl.when(z > 0)
+            @pl.when(has_down(c))
             def _():
                 go_down(z + d, c).start()
 
@@ -196,26 +222,20 @@
 
     rden[...] = 1.0 / rden[...]
 
-    pltpu.make_async_copy(qs, qs, ld_misc.at[2]).wait()
     pltpu.make_async_copy(rs, rs, ld_misc.at[3]).wait()
 
     first_head = lax.broadcasted_iota(jnp.int32, (tokens, LANES), 1) < HEAD_DIM
     keys = rows * tokens
 
-    for c in range(chunks):
-        relay(chips - 1, c)
-
-        @pl.loop(0, chips)
-        def _(chip, c=c):
-            wait_slot(chip, 1 - core, c)
-
-        q = qs[c]
-        none = jnp.zeros_like(q)
-        q2 = jnp.concatenate(
-            [jnp.where(first_head, q, none), jnp.where(first_head, none, q)], axis=0
+    def attend(blocks, c):
+        none = jnp.zeros_like(blocks[0])
+        queries = jnp.concatenate(
+            [part for q in blocks
+             for part in (jnp.where(first_head, q, none), jnp.where(first_head, none, q))],
+            axis=0,
         )
         scores = lax.dot_general(
-            q2, kv[:, c, 0].reshape(keys, LANES), (((1,), (1,)), ((), ())),
+            queries, kv[:, c, 0].reshape(keys, LANES), (((1,), (1,)), ((), ())),
             preferred_element_type=jnp.float32,
         )
         top = jnp.max(scores, axis=1, keepdims=True)
@@ -225,9 +245,44 @@
             raised.astype(jnp.bfloat16), kv[:, c, 1].reshape(keys, LANES),
             preferred_element_type=jnp.float32,
         ) / denom
-        spatial = jnp.where(first_head, both[:tokens], both[tokens:]).astype(jnp.bfloat16)
-        sob[c] = spatial
-        hb[me_f, c] = (rs[c].astype(jnp.float32) + spatial.astype(jnp.float32)).astype(jnp.bfloat16)
+        return [
+            jnp.where(
+                first_head,
+                both[2 * i * tokens : (2 * i + 1) * tokens],
+                both[(2 * i + 1) * tokens : (2 * i + 2) * tokens],
+            ).astype(jnp.bfloat16)
+            for i in range(len(blocks))
+        ]
+
+    for c in range(chunks):
+        relay(chips - 1, c)
+
+        @pl.when(attends(c))
+        def _(c=c):
+            @pl.loop(0, chips)
+            def _(chip):
+                wait_slot(chip, 1 - core, c)
+
+        if c < lent:
+            @pl.when(helps)
+            def _(c=c):
+                if c == 0:
+                    lend().wait_recv()
+                sob[c], oh[c] = attend([qs[c], qh[c]], c)
+                give_back(c).start()
+
+            @pl.when(at_end)
+            def _(c=c):
+                give_back(c).wait_recv()
+
+            if chips > 4:
+                @pl.when(jnp.logical_not(jnp.logical_or(at_end, helps)))
+                def _(c=c):
+                    sob[c] = attend([qs[c]], c)[0]
+        else:
+            sob[c] = attend([qs[c]], c)[0]
+
+        hb[me_f, c] = (rs[c].astype(jnp.float32) + sob[c].astype(jnp.float32)).astype(jnp.bfloat16)
 
         @pl.loop(me_f + 1, frames)
         def _(to, c=c):
@@ -300,13 +355,15 @@
     @pl.loop(0, chips)
     def _(chip):
         for c in range(chunks):
-            to_partner(chip, c).wait_send()
-
-            @pl.when(jnp.logical_and(chip <= z, z < chips - 1))
+            @pl.when(attends(c))
+            def _(c=c):
+                to_partner(chip, c).wait_send()
+
+            @pl.when(jnp.logical_and(jnp.logical_and(chip <= z, has_up(c)), jnp.logical_or(attends(c), chip == z)))
             def _(c=c):
                 go_up(chip, c).wait_send()
 
-            @pl.when(jnp.logical_and(chip >= z, z > 0))
+            @pl.when(jnp.logical_and(jnp.logical_and(chip >= z, has_down(c)), jnp.logical_or(attends(c), chip == z)))
             def _(c=c):
                 go_down(chip, c).wait_send()
 
@@ -325,6 +382,16 @@
         def _(c=c):
             halo_copy(1, c).wait_send()
 
+    if lent:
+        @pl.when(at_end)
+        def _():
+            lend().wait_send()
+
+    for c in range(lent):
+        @pl.when(helps)
+        def _(c=c):
+            give_back(c).wait_send()
+
     pltpu.make_async_copy(sob, sob, out_sem.at[0]).wait()
     pltpu.make_async_copy(bob, bob, out_sem.at[1]).wait()
 
@@ -334,19 +401,23 @@
     _, _, tokens, channels = block.shape
     chunks = channels // LANES
     chips = rows // 2
+    lent = chunks // 2 if chips >= 4 else 0
+    held = max(lent, 1)
     slab = (chunks, tokens, LANES)
     flat = (chunks * tokens, LANES)
     bf16, f32 = jnp.bfloat16, jnp.float32
     dma = pltpu.SemaphoreType.DMA
     anywhere = pl.BlockSpec(memory_space=pl.ANY)
     return pl.pallas_call(
-        functools.partial(block_kernel, frames, rows, chunks, tokens),
+        functools.partial(block_kernel, frames, rows, chunks, tokens, lent),
         out_shape=(jax.ShapeDtypeStruct(block.shape, bf16),) * 2,
         in_specs=[anywhere] * 8,
         out_specs=(anywhere, anywhere),
         scratch_shapes=[
             pltpu.VMEM((rows, chunks, 2, tokens, LANES), bf16),
             pltpu.VMEM(slab, bf16),
+            pltpu.VMEM((held,) + slab[1:], bf16),
+            pltpu.VMEM((held,) + slab[1:], bf16),
             pltpu.VMEM(slab, bf16),
             pltpu.VMEM(slab, bf16),
             pltpu.VMEM((frames,) + slab, bf16),
@@ -364,6 +435,7 @@
             dma((chips, chunks)), dma((chips, chunks)), dma((chips, chunks)),
             dma((frames,)), dma((frames,)), dma((frames, chunks)), dma((frames, chunks)),
             dma((2, chunks)), dma((2, chunks)), dma((2,)),
+            dma((2,)), dma((held,)), dma((held,)),
         ],
         compiler_params=pltpu.CompilerParams(collective_id=0, has_side_effects=True),
         name="block",

time: 33.6 us -> 32.3 us (0.961)
  the two profiles are of different devices: /device:TPU:23 before, /device:TPU:12 now
where the time goes in v2:
time: 32.3 us; the launch traced here: 32.1 us
  Pallas kernels  29.2 us (90%)
  local copies, waits for them, and re-layouts  2.22 us (7%)
  between operations  0.65 us (2%)
    pallas_call x1, Pallas kernels, on_device(): pl.pallas_call(functools.partial(block_kernel, frames, rows, chunks, toke...  29.2 us
    unnamed x4, local copies, waits for them, and re-layouts  2.22 us

profile of v2, /device:TPU:12, one launch (start us, length us, event | category | flops | bytes accessed | tf_op | source)
XLA Modules:
  0.0 32.1 jit_solution(11467875972624970892)
XLA Ops:
  0.6 29.2 %block.1 = (bf16[1,1,64,768]{3,2,1,0:T(8,128)(2,1)}, bf16[1,1,64,768]{3,2,1,0:T(8,128)(2,1)}) custom-call(bf16[1,1,64,768]{3,2,1,0:T(8,128)(2,1)} %res_hbm.1, bf16[1,1,64,768]{3,2,1,0:T(8,128)(2,1)} %q_hbm.1, bf16[1,1,64,768]{3,2,1,0:T(8,128)(2,1)} %k_hbm.1, bf16[1,1,64,768]{3,2,1,0:T(8,128)(2,1)} %v_hbm.1, bf16[1,1,64,768]{3,2,1,0:T(8,128)(2,1)} %qt_hbm.1, ...), custom_call_target="tpu_custom_call" | custom-call | tf_op jit(solution)/shard_map/block/pallas_call | solution.py:411
  29.8 0.0 copy-start
  29.9 1.6 %copy.12 = bf16[1,1,64,768]{3,2,1,0:T(8,128)(2,1)} copy(bf16[1,1,64,768]{3,2,1,0:T(8,128)(2,1)} %get-tuple-element.4) | data formatting | bytes 196608
  31.4 0.0 copy-done
  31.4 0.6 %copy.13 = bf16[1,1,64,768]{3,2,1,0:T(8,128)(2,1)} copy(bf16[1,1,64,768]{3,2,1,0:T(8,128)(2,1)S(1)} %copy-done) | data formatting | bytes 196608
Async XLA Ops:
  29.8 1.6 %copy-start = (bf16[1,1,64,768]{3,2,1,0:T(8,128)(2,1)S(1)}, bf16[1,1,64,768]{3,2,1,0:T(8,128)(2,1)}, u32[]{:S(2)}) copy-start(bf16[1,1,64,768]{3,2,1,0:T(8,128)(2,1)} %get-tuple-element.5) | copy-start | bytes 294916

commit v3 on v2

--- a/solution.py
+++ b/solution.py
@@ -102,26 +102,26 @@
         return remote(kv.at[src, c], kv.at[src, c], send, kv_recv.at[src, c], row=to_row)
 
     def go_up(chip, c):
-        return kv_copy(chip, core, c, up_send.at[chip, c], me_r + 2)
+        return kv_copy(chip, core, c, up_send.at[chip], me_r + 2)
 
     def go_down(chip, c):
-        return kv_copy(chip, core, c, dn_send.at[chip, c], me_r - 2)
+        return kv_copy(chip, core, c, dn_send.at[chip], me_r - 2)
 
     def to_partner(chip, c):
-        return kv_copy(chip, core, c, pt_send.at[chip, c], me_r + 1 - 2 * core)
+        return kv_copy(chip, core, c, pt_send.at[chip], me_r + 1 - 2 * core)
 
     def wait_slot(chip, of_core, c):
-        kv_copy(chip, of_core, c, up_send.at[chip, c], me_r + 1 - 2 * core).wait_recv()
+        kv_copy(chip, of_core, c, up_send.at[chip], me_r + 1 - 2 * core).wait_recv()
 
     def kt_copy(g, to):
         return remote(ktb.at[g], ktb.at[g], kt_send.at[to], kt_recv.at[g], frame=to)
 
     def h_copy(g, to, c):
-        return remote(hb.at[g, c], hb.at[g, c], h_send.at[to, c], h_recv.at[g, c], frame=to)
+        return remote(hb.at[g, c], hb.at[g, c], h_send.at[to], h_recv.at[g, c], frame=to)
 
     def halo_copy(side, c):
         return remote(
-            mixb.at[1, c], mixb.at[2 - 2 * side, c], halo_send.at[side, c],
+            mixb.at[1, c], mixb.at[2 - 2 * side, c], halo_send.at[side],
             halo_recv.at[1 - side, c], row=me_r - 1 + 2 * side,
         )
 
@@ -179,48 +179,12 @@
 
             to_partner(z + d, c).start()
 
-    @pl.loop(1, chips - 1)
+    last = jnp.maximum(z, chips - 1 - z)
+
+    @pl.loop(1, last)
     def _(d):
         for c in range(chunks):
             relay(d, c)
-
-    pltpu.make_async_copy(qts, qts, ld_misc.at[1]).wait()
-
-    @pl.loop(0, me_f)
-    def _(g):
-        kt_copy(g, me_f).wait_recv()
-
-    flat = chunks * tokens
-    same = (
-        (lax.broadcasted_iota(jnp.int32, (2 * LANES, LANES), 0) // HEAD_DIM) % 2
-        == lax.broadcasted_iota(jnp.int32, (2 * LANES, LANES), 1) // HEAD_DIM
-    )
-    spread = jnp.where(same, 1.0, 0.0).astype(jnp.bfloat16)
-    peak[...] = jnp.full(peak.shape, -1e30, jnp.float32)
-
-    @pl.loop(0, me_f + 1)
-    def _(g):
-        product = (
-            qts[...].reshape(flat, LANES).astype(jnp.float32)
-            * ktb[g].reshape(flat, LANES).astype(jnp.float32)
-        )
-        high = product.astype(jnp.bfloat16)
-        low = (product - high.astype(jnp.float32)).astype(jnp.bfloat16)
-        score = jnp.dot(
-            jnp.concatenate([high, low], axis=1), spread, preferred_element_type=jnp.float32
-        )
-        tsc[g] = score
-        peak[...] = jnp.maximum(peak[...], score)
-
-    rden[...] = jnp.zeros(rden.shape, jnp.float32)
-
-    @pl.loop(0, me_f + 1)
-    def _(g):
-        raised = jnp.exp2((tsc[g] - peak[...]) * (SCALE * LOG2E))
-        rden[...] += raised
-        wts[g] = raised.astype(jnp.bfloat16)
-
-    rden[...] = 1.0 / rden[...]
 
     pltpu.make_async_copy(rs, rs, ld_misc.at[3]).wait()
 
@@ -255,7 +219,7 @@
         ]
 
     for c in range(chunks):
-        relay(chips - 1, c)
+        relay(last, c)
 
         @pl.when(attends(c))
         def _(c=c):
@@ -290,6 +254,44 @@
 
         pltpu.make_async_copy(sob.at[c], so_hbm.at[0, 0, :, lanes(c)], out_sem.at[0]).start()
 
+    pltpu.make_async_copy(qts, qts, ld_misc.at[1]).wait()
+
+    @pl.loop(0, me_f)
+    def _(g):
+        kt_copy(g, me_f).wait_recv()
+
+    flat = chunks * tokens
+    same = (
+        (lax.broadcasted_iota(jnp.int32, (2 * LANES, LANES), 0) // HEAD_DIM) % 2
+        == lax.broadcasted_iota(jnp.int32, (2 * LANES, LANES), 1) // HEAD_DIM
+    )
+    spread = jnp.where(same, 1.0, 0.0).astype(jnp.bfloat16)
+    peak[...] = jnp.full(peak.shape, -1e30, jnp.float32)
+
+    @pl.loop(0, me_f + 1)
+    def _(g):
+        product = (
+            qts[...].reshape(flat, LANES).astype(jnp.float32)
+            * ktb[g].reshape(flat, LANES).astype(jnp.float32)
+        )
+        high = product.astype(jnp.bfloat16)
+        low = (product - high.astype(jnp.float32)).astype(jnp.bfloat16)
+        score = jnp.dot(
+            jnp.concatenate([high, low], axis=1), spread, preferred_element_type=jnp.float32
+        )
+        tsc[g] = score
+        peak[...] = jnp.maximum(peak[...], score)
+
+    rden[...] = jnp.zeros(rden.shape, jnp.float32)
+
+    @pl.loop(0, me_f + 1)
+    def _(g):
+        raised = jnp.exp2((tsc[g] - peak[...]) * (SCALE * LOG2E))
+        rden[...] += raised
+        wts[g] = raised.astype(jnp.bfloat16)
+
+    rden[...] = 1.0 / rden[...]
+
     for c in range(chunks):
         @pl.loop(0, me_f)
         def _(g, c=c):
@@ -330,14 +332,14 @@
         @pl.when(me_r > 0)
         def _(c=c):
             remote(
-                mixb.at[0, c], mixb.at[0, c], halo_send.at[0, c], halo_recv.at[0, c],
+                mixb.at[0, c], mixb.at[0, c], halo_send.at[0], halo_recv.at[0, c],
                 row=me_r - 1,
             ).wait_recv()
 
         @pl.when(me_r < rows - 1)
         def _(c=c):
             remote(
-                mixb.at[2, c], mixb.at[2, c], halo_send.at[1, c], halo_recv.at[1, c],
+                mixb.at[2, c], mixb.at[2, c], halo_send.at[1], halo_recv.at[1, c],
                 row=me_r + 1,
             ).wait_recv()
 
@@ -352,35 +354,57 @@
         bob[c] = (lines[1] + 0.5 * conv * (1.0 + jnp.tanh(inner))).astype(jnp.bfloat16)
         pltpu.make_async_copy(bob.at[c], bo_hbm.at[0, 0, :, lanes(c)], out_sem.at[1]).start()
 
+    def drain(ref, sem):
+        pltpu.make_async_copy(ref, ref, sem).wait()
+
+    some = pl.ds(lent, chunks - lent)
+
     @pl.loop(0, chips)
     def _(chip):
-        for c in range(chunks):
-            @pl.when(attends(c))
-            def _(c=c):
-                to_partner(chip, c).wait_send()
-
-            @pl.when(jnp.logical_and(jnp.logical_and(chip <= z, has_up(c)), jnp.logical_or(attends(c), chip == z)))
-            def _(c=c):
-                go_up(chip, c).wait_send()
-
-            @pl.when(jnp.logical_and(jnp.logical_and(chip >= z, has_down(c)), jnp.logical_or(attends(c), chip == z)))
-            def _(c=c):
-                go_down(chip, c).wait_send()
+        src = 2 * chip + core
+
+        @pl.when(at_end)
+        def _():
+            drain(kv.at[src, some], pt_send.at[chip])
+
+        @pl.when(jnp.logical_not(at_end))
+        def _():
+            drain(kv.at[src], pt_send.at[chip])
+
+    bound = 1 if lent else 0
+
+    @pl.loop(0, z + 1)
+    def _(chip):
+        @pl.when(z < chips - 1 - bound)
+        def _():
+            drain(kv.at[2 * chip + core], up_send.at[chip])
+
+        @pl.when(jnp.logical_and(z < chips - 1, z >= chips - 1 - bound))
+        def _():
+            drain(kv.at[2 * chip + core, some], up_send.at[chip])
+
+    @pl.loop(z, chips)
+    def _(chip):
+        @pl.when(z > bound)
+        def _():
+            drain(kv.at[2 * chip + core], dn_send.at[chip])
+
+        @pl.when(jnp.logical_and(z > 0, z <= bound))
+        def _():
+            drain(kv.at[2 * chip + core, some], dn_send.at[chip])
 
     @pl.loop(me_f + 1, frames)
     def _(to):
         kt_copy(me_f, to).wait_send()
-        for c in range(chunks):
-            h_copy(me_f, to, c).wait_send()
-
-    for c in range(chunks):
-        @pl.when(me_r > 0)
-        def _(c=c):
-            halo_copy(0, c).wait_send()
-
-        @pl.when(me_r < rows - 1)
-        def _(c=c):
-            halo_copy(1, c).wait_send()
+        drain(hb.at[me_f], h_send.at[to])
+
+    @pl.when(me_r > 0)
+    def _():
+        drain(mixb.at[1], halo_send.at[0])
+
+    @pl.when(me_r < rows - 1)
+    def _():
+        drain(mixb.at[1], halo_send.at[1])
 
     if lent:
         @pl.when(at_end)
@@ -401,7 +425,7 @@
     _, _, tokens, channels = block.shape
     chunks = channels // LANES
     chips = rows // 2
-    lent = chunks // 2 if chips >= 4 else 0
+    lent = chunks * 3 // 6 if chips >= 4 else 0
     held = max(lent, 1)
     slab = (chunks, tokens, LANES)
     flat = (chunks * tokens, LANES)
@@ -432,14 +456,15 @@
             pltpu.VMEM(args[6].shape, f32),
             pltpu.VMEM(args[7].shape, f32),
             dma((chunks,)), dma((6,)), dma((rows, chunks)),
-            dma((chips, chunks)), dma((chips, chunks)), dma((chips, chunks)),
-            dma((frames,)), dma((frames,)), dma((frames, chunks)), dma((frames, chunks)),
-            dma((2, chunks)), dma((2, chunks)), dma((2,)),
+            dma((chips,)), dma((chips,)), dma((chips,)),
+            dma((frames,)), dma((frames,)), dma((frames, chunks)), dma((frames,)),
+            dma((2, chunks)), dma((2,)), dma((2,)),
             dma((2,)), dma((held,)), dma((held,)),
         ],
-        compiler_params=pltpu.CompilerParams(collective_id=0, has_side_effects=True),
+        compiler_params=pltpu.CompilerParams(collective_id=0, has_side_effects=True,
+            vmem_limit_bytes=(14 << 20) + (rows << 18) + (frames << 19)),
         name="block",
-    )(*args)
+    )(*[pltpu.with_memory_space_constraint(a, pltpu.HBM) for a in args])
 
 
 def solution(mesh):

time: 32.3 us -> 30.1 us (0.932)
  the two profiles are of different devices: /device:TPU:12 before, /device:TPU:7 now
where the time goes in v3:
time: 30.1 us; the launch traced here: 30 us
  Pallas kernels  28 us (93%)
  local copies, waits for them, and re-layouts  1.28 us (4%)
  between operations  0.64 us (2%)
    pallas_call x1, Pallas kernels, on_device(): pl.pallas_call(functools.partial(block_kernel, frames, rows, chunks, toke...  28 us
    unnamed x2, local copies, waits for them, and re-layouts  1.28 us

profile of v3, /device:TPU:7, one launch (start us, length us, event | category | flops | bytes accessed | tf_op | source)
XLA Modules:
  0.0 30.0 jit_solution(6015188699920772573)
XLA Ops:
  0.6 28.0 %block.1 = (bf16[1,1,64,768]{3,2,1,0:T(8,128)(2,1)S(1)}, bf16[1,1,64,768]{3,2,1,0:T(8,128)(2,1)S(1)}) custom-call(bf16[1,1,64,768]{3,2,1,0:T(8,128)(2,1)} %res_hbm.1, bf16[1,1,64,768]{3,2,1,0:T(8,128)(2,1)} %q_hbm.1, bf16[1,1,64,768]{3,2,1,0:T(8,128)(2,1)} %k_hbm.1, bf16[1,1,64,768]{3,2,1,0:T(8,128)(2,1)} %v_hbm.1, bf16[1,1,64,768]{3,2,1,0:T(8,128)(2,1)} %qt_hbm.1, ...), custom_call_target="tpu_custom_call" | custom-call | tf_op jit(solution)/shard_map/block/pallas_call | solution.py:435
  28.7 0.6 %copy.12 = bf16[1,1,64,768]{3,2,1,0:T(8,128)(2,1)} copy(bf16[1,1,64,768]{3,2,1,0:T(8,128)(2,1)S(1)} %get-tuple-element.4) | data formatting | bytes 196608
  29.3 0.6 %copy.13 = bf16[1,1,64,768]{3,2,1,0:T(8,128)(2,1)} copy(bf16[1,1,64,768]{3,2,1,0:T(8,128)(2,1)S(1)} %get-tuple-element.5) | data formatting | bytes 196608

commit v4 on v3

--- a/solution.py
+++ b/solution.py
@@ -219,7 +219,10 @@
         ]
 
     for c in range(chunks):
-        relay(last, c)
+        if c == 0:
+            relay(last, 0)
+        if c + 1 < chunks:
+            relay(last, c + 1)
 
         @pl.when(attends(c))
         def _(c=c):

time: 30.1 us -> 27.2 us (0.904)
  the two profiles are of different devices: /device:TPU:7 before, /device:TPU:12 now
where the time goes in v4:
time: 27.2 us; the launch traced here: 27 us
  Pallas kernels  25.1 us (92%)
  local copies, waits for them, and re-layouts  1.28 us (5%)
  between operations  0.64 us (2%)
    pallas_call x1, Pallas kernels, on_device(): pl.pallas_call(functools.partial(block_kernel, frames, rows, chunks, toke...  25.1 us
    unnamed x2, local copies, waits for them, and re-layouts  1.28 us

profile of v4, /device:TPU:12, one launch (start us, length us, event | category | flops | bytes accessed | tf_op | source)
XLA Modules:
  0.0 27.0 jit_solution(313656160889678151)
XLA Ops:
  0.6 25.1 %block.1 = (bf16[1,1,64,768]{3,2,1,0:T(8,128)(2,1)S(1)}, bf16[1,1,64,768]{3,2,1,0:T(8,128)(2,1)S(1)}) custom-call(bf16[1,1,64,768]{3,2,1,0:T(8,128)(2,1)} %res_hbm.1, bf16[1,1,64,768]{3,2,1,0:T(8,128)(2,1)} %q_hbm.1, bf16[1,1,64,768]{3,2,1,0:T(8,128)(2,1)} %k_hbm.1, bf16[1,1,64,768]{3,2,1,0:T(8,128)(2,1)} %v_hbm.1, bf16[1,1,64,768]{3,2,1,0:T(8,128)(2,1)} %qt_hbm.1, ...), custom_call_target="tpu_custom_call" | custom-call | tf_op jit(solution)/shard_map/block/pallas_call | solution.py:438
  25.7 0.6 %copy.12 = bf16[1,1,64,768]{3,2,1,0:T(8,128)(2,1)} copy(bf16[1,1,64,768]{3,2,1,0:T(8,128)(2,1)S(1)} %get-tuple-element.4) | data formatting | bytes 196608
  26.4 0.6 %copy.13 = bf16[1,1,64,768]{3,2,1,0:T(8,128)(2,1)} copy(bf16[1,1,64,768]{3,2,1,0:T(8,128)(2,1)S(1)} %get-tuple-element.5) | data formatting | bytes 196608
